TPU v7x, 128 devices: a whole 4x4x4 slice. The times are simulated.
128 devices in a mesh: ctx: 16 (over y_hi, z, core), head: 8 (over y_lo, x).
Axes of the slice: x: 4, y: 4 (y_hi: 2, y_lo: 2; y = y_hi * 2 + y_lo), z: 4, core: 2. Of those that a mesh axis runs over, the one named last changes fastest.
Arguments:
- queries: bfloat16 [16384, 4096], P('ctx', 'head'), may hold values from -24 to 24
- key_states: bfloat16 [16384, 4096], P('ctx', 'head'), may hold values from -24 to 24
- value_states: bfloat16 [16384, 4096], P('ctx', 'head'), may hold values from -6 to 6
- out_grad: bfloat16 [16384, 4096], P('ctx', 'head'), may hold values from -6 to 6
- selected: int32 [256, 16], P('ctx'), may hold values from -1 to 255, as said below
Outputs:
- query_grad: bfloat16 [16384, 4096], P(('ctx', 'head'))
- key_grad: bfloat16 [16384, 4096], P(('ctx', 'head'))
- value_grad: bfloat16 [16384, 4096], P(('ctx', 'head'))
Inputs may be any that keep to these rules, and one draw needn't show every extreme that they name: `selected`: row i holds 16 distinct entries, each a block index or -1; block i itself is always among them and every other block named comes before i. In the aligned groups of 16 rows, the blocks named that lie in another group's range number at most 1 for each other group, exactly 1 for every earlier group, and none for a later group.
All inputs are finite; a program needn't handle non-finite values.
Results may differ from a plain program's by a relative error of at most 0.011.
Values may be sent and summed in bfloat16 or wider, within the bound.
No kernel may reach another device: no remote copies, remote signals or barrier semaphores. Data moves between devices by JAX's collectives and lax.ppermute only.
A program may use at most 192 MiB of HBM per device.

v0:
```python
import jax
import jax.numpy as jnp
from jax import lax
from jax.sharding import PartitionSpec as P

HDIM = 128
HEAD_DEV = 4
BLOCK = 64
TOPK = 16
CAP = 1
GROUP = 8


def pack_slots(member, ranking, per_dev):
    slots = jnp.arange(CAP, dtype=jnp.int32)
    locals_idx = jnp.arange(per_dev, dtype=jnp.int32)
    picks = member[:, None, :] & (ranking[:, None, :] == slots[None, :, None])
    return jnp.sum(jnp.where(picks, locals_idx[None, None, :], 0), axis=2)


def group_grads(query_blk, key_blk, value_blk, grad_blk, select_blk, own_ids):
    count = query_blk.shape[0]
    scale = 1.0 / HDIM**0.5
    width = HEAD_DEV * HDIM
    query_h = query_blk.reshape(count, BLOCK, HEAD_DEV, HDIM)
    key_h = key_blk.reshape(count, TOPK * BLOCK, HEAD_DEV, HDIM)
    value_h = value_blk.reshape(count, TOPK * BLOCK, HEAD_DEV, HDIM)
    grad_h = grad_blk.reshape(count, BLOCK, HEAD_DEV, HDIM)
    key_idx = jnp.arange(TOPK * BLOCK, dtype=jnp.int32)
    slot_of = key_idx // BLOCK
    key_pos = key_idx % BLOCK
    query_pos = jnp.arange(BLOCK, dtype=jnp.int32)
    block_of = select_blk[:, slot_of]
    allowed = (block_of >= 0)[:, None, :] & (
        (block_of != own_ids[:, None])[:, None, :]
        | (key_pos[None, None, :] <= query_pos[None, :, None])
    )
    scores = (
        jnp.einsum("gqhd,gkhd->ghqk", query_h, key_h, preferred_element_type=jnp.float32) * scale
    )
    scores = jnp.where(allowed[:, None], scores, -1e30)
    highest = jnp.max(scores, axis=-1, keepdims=True)
    expo = jnp.exp(scores - highest)
    probs = expo / jnp.sum(expo, axis=-1, keepdims=True)
    probs_low = probs.astype(jnp.bfloat16)
    output = jnp.einsum("ghqk,gkhd->gqhd", probs_low, value_h, preferred_element_type=jnp.float32)
    delta = jnp.einsum("gqhd,gqhd->ghq", grad_h.astype(jnp.float32), output)
    dprobs = jnp.einsum("gqhd,gkhd->ghqk", grad_h, value_h, preferred_element_type=jnp.float32)
    dscores = probs * (dprobs - delta[..., None])
    dscores_low = dscores.astype(jnp.bfloat16)
    dquery = (
        jnp.einsum("ghqk,gkhd->gqhd", dscores_low, key_h, preferred_element_type=jnp.float32)
        * scale
    ).astype(jnp.bfloat16)
    dkey = (
        jnp.einsum("ghqk,gqhd->gkhd", dscores_low, query_h, preferred_element_type=jnp.float32)
        * scale
    )
    dvalue = jnp.einsum("ghqk,gqhd->gkhd", probs_low, grad_h, preferred_element_type=jnp.float32)
    return (
        dquery.reshape(count, BLOCK, width),
        dkey.reshape(count * TOPK, BLOCK, width),
        dvalue.reshape(count * TOPK, BLOCK, width),
    )


def per_device(queries, key_states, value_states, out_grad, selected):
    ranges = lax.axis_size("ctx")
    here = lax.axis_index("ctx")
    per_dev = selected.shape[0]
    width = queries.shape[1]
    range_ids = jnp.arange(ranges, dtype=jnp.int32)
    locals_idx = jnp.arange(per_dev, dtype=jnp.int32)
    usable = selected >= 0
    owner = jnp.where(usable, selected // per_dev, here)
    local_blk = jnp.where(usable, selected % per_dev, 0)
    hits = (owner[:, :, None, None] == range_ids[None, None, :, None]) & (
        local_blk[:, :, None, None] == locals_idx[None, None, None, :]
    )
    remote = usable & (owner != here)
    member = jnp.any(hits & remote[:, :, None, None], axis=(0, 1))
    ranking = jnp.cumsum(member.astype(jnp.int32), axis=1) - 1
    wanted_ids = pack_slots(member, ranking, per_dev)
    asks = lax.all_to_all(wanted_ids, "ctx", split_axis=0, concat_axis=0, tiled=True)
    key_blocks = key_states.reshape(per_dev, BLOCK, width)
    value_blocks = value_states.reshape(per_dev, BLOCK, width)
    sent_keys = key_blocks[asks]
    sent_values = value_blocks[asks]
    got_keys, got_values = (
        lax.all_to_all(sent_keys, "ctx", split_axis=0, concat_axis=0, tiled=True),
        lax.all_to_all(sent_values, "ctx", split_axis=0, concat_axis=0, tiled=True),
    )
    bank_keys = jnp.concatenate([key_blocks, got_keys.reshape(ranges * CAP, BLOCK, width)], axis=0)
    bank_values = jnp.concatenate(
        [value_blocks, got_values.reshape(ranges * CAP, BLOCK, width)], axis=0
    )
    rank_sel = jnp.sum(jnp.where(hits, ranking[None, None], 0), axis=(2, 3))
    bank_index = jnp.where(owner == here, local_blk, per_dev + owner * CAP + rank_sel)
    steps = per_dev // GROUP
    own_all = (here * per_dev + locals_idx).reshape(steps, GROUP)
    inputs = (
        queries.reshape(steps, GROUP, BLOCK, width),
        out_grad.reshape(steps, GROUP, BLOCK, width),
        bank_index.reshape(steps, GROUP, TOPK),
        selected.reshape(steps, GROUP, TOPK),
        own_all,
    )

    def advance(carry, item):
        grad_keys, grad_values = carry
        query_c, grad_c, index_c, select_c, own_c = item
        key_c = bank_keys[index_c].reshape(GROUP, TOPK * BLOCK, width)
        value_c = bank_values[index_c].reshape(GROUP, TOPK * BLOCK, width)
        dquery, dkey, dvalue = group_grads(query_c, key_c, value_c, grad_c, select_c, own_c)
        flat = index_c.reshape(-1)
        return ((grad_keys.at[flat].add(dkey), grad_values.at[flat].add(dvalue)), dquery)

    zeros = jnp.zeros((per_dev + ranges * CAP, BLOCK, width), jnp.float32)
    (grad_keys, grad_values), dquery = lax.scan(advance, (zeros, zeros), inputs)
    query_local = dquery.reshape(per_dev * BLOCK, width)
    back_keys, back_values = (
        lax.all_to_all(
            grad_keys[per_dev:].reshape(ranges, CAP, BLOCK, width),
            "ctx",
            split_axis=0,
            concat_axis=0,
            tiled=True,
        ),
        lax.all_to_all(
            grad_values[per_dev:].reshape(ranges, CAP, BLOCK, width),
            "ctx",
            split_axis=0,
            concat_axis=0,
            tiled=True,
        ),
    )
    flat_asks = asks.reshape(-1)
    key_total = grad_keys[:per_dev].at[flat_asks].add(back_keys.reshape(ranges * CAP, BLOCK, width))
    value_total = (
        grad_values[:per_dev].at[flat_asks].add(back_values.reshape(ranges * CAP, BLOCK, width))
    )
    key_local = key_total.reshape(per_dev * BLOCK, width).astype(jnp.bfloat16)
    value_local = value_total.reshape(per_dev * BLOCK, width).astype(jnp.bfloat16)
    query_out, key_out, value_out = (
        lax.all_to_all(query_local, "head", split_axis=0, concat_axis=1, tiled=True),
        lax.all_to_all(key_local, "head", split_axis=0, concat_axis=1, tiled=True),
        lax.all_to_all(value_local, "head", split_axis=0, concat_axis=1, tiled=True),
    )
    return (query_out, key_out, value_out)


def solution(mesh):
    return jax.shard_map(
        per_device,
        mesh=mesh,
        in_specs=(
            P("ctx", "head"),
            P("ctx", "head"),
            P("ctx", "head"),
            P("ctx", "head"),
            P("ctx", None),
        ),
        out_specs=(P(("ctx", "head"), None), P(("ctx", "head"), None), P(("ctx", "head"), None)),
        check_vma=False,
    )
```

profile of v0, /device:TPU:1, one launch (start us, length us, event | category | flops | bytes accessed | tf_op | source)
XLA Modules:
  0.0 779.9 jit_solution(9552881560634844395)
XLA Ops:
  3.8 16.2 %all_to_all.83 = s32[16,1,1]{2,1,0:T(1,128)S(1)} all-to-all(s32[16,1,1]{2,1,0:T(1,128)S(1)} %copy.83), channel_id=1, replica_groups=mesh['ctx'=16,'head'=8] {'ctx'}, dimensions={0} | all-to-all | bytes 128 | tf_op jit(solution)/shard_map/all_to_all | solution.py:84
  21.2 2.8 gather_fusion.3
  24.0 4.1 all-to-all-start.1
  28.1 2.8 gather_fusion.4
  30.9 14.5 %all-to-all-done.1 = bf16[16,1,64,512]{3,2,1,0:T(8,128)(2,1)S(1)} async-done(((bf16[16,1,64,512]{3,2,1,0:T(8,128)(2,1)}), bf16[16,1,64,512]{3,2,1,0:T(8,128)(2,1)S(1)}, u32[]{:S(2)}, u32[]{:S(2)}) %all-to-all-start.1) | async-done | bytes 1048608 | tf_op jit(solution)/shard_map/all_to_all | solution.py:90
  45.4 5.0 all-to-all-start.2
  50.4 5.4 fusion.47
  57.2 10.6 %all-to-all-done.2 = bf16[16,1,64,512]{3,2,1,0:T(8,128)(2,1)} async-done(((bf16[16,1,64,512]{3,2,1,0:T(8,128)(2,1)}), bf16[16,1,64,512]{3,2,1,0:T(8,128)(2,1)}, u32[]{:S(2)}, u32[]{:S(2)}) %all-to-all-start.2) | async-done | bytes 1048608 | tf_op jit(solution)/shard_map/all_to_all | solution.py:91
  67.8 3.1 pad_maximum_fusion.1
  70.8 2.4 broadcast_in_dim.72.clone
  73.3 2.5 broadcast_in_dim.72
  75.8 567.8 %while.16 = (s32[]{:T(128)}, f32[32,64,512]{2,1,0:T(8,128)}, f32[32,64,512]{2,1,0:T(8,128)}, bf16[2,8,64,512]{3,2,1,0:T(8,128)(2,1)}, s32[2,8,16]{2,1,0:T(8,128)...) while((s32[]{:T(128)}, f32[32,64,512]{2,1,0:T(8,128)}, ...), condition=%wide.region_9.10_spmd, body=%wide.region_4.9_spmd.sunk | while | flops 3265628928 | bytes 477484352 | solution.py:119
  93.3 2.8 gather_fusion.2
  97.7 2.1 constant_dynamic-slice_fusion.6
  102.2 6.3 gather_fusion.1
  108.5 12.5 %reshape.486 = bf16[8,1024,4,128]{3,2,1,0:T(4,128)(2,1)} reshape(bf16[128,64,512]{2,1,0:T(8,128)(2,1)} %gather_fusion.1) | data formatting | bytes 16777216 | tf_op jit(solution)/shard_map/while/body/eval_jaxpr/reshape;while/body/eval_jaxpr/reshape | solution.py:26
  121.0 7.9 %gather_fusion = bf16[128,64,512]{2,1,0:T(8,128)(2,1)} fusion(bf16[32,64,512]{2,1,0:T(8,128)(2,1)} %get-tuple-element.313, s32[1024]{0:T(1024)S(1)} %pad_clamp_fusion.3), kind=kCustom, calls=%fused_computation.2.clone.1 | custom fusion | bytes 16777728 | tf_op jit(solution)/shard_map/while/body/eval_jaxpr/gather | solution.py:113
  129.0 12.5 %reshape.484 = bf16[8,1024,4,128]{3,2,1,0:T(4,128)(2,1)} reshape(bf16[128,64,512]{2,1,0:T(8,128)(2,1)} %gather_fusion) | data formatting | bytes 16777216 | tf_op jit(solution)/shard_map/while/body/eval_jaxpr/reshape;while/body/eval_jaxpr/reshape | solution.py:27
  141.5 9.8 %fusion.90 = f32[8,4,64,1024]{3,2,1,0:T(8,128)} fusion(bf16[8,1024,4,128]{3,2,1,0:T(4,128)(2,1)} %reshape.486, bf16[8,64,4,128]{3,2,1,0:T(4,128)(2,1)S(1)} %reshape.487), kind=kOutput, calls=%fused_computation.21.clone.1 | convolution fusion | flops 536870912 | bytes 17301504 | tf_op jit(solution)/shard_map/while/body/eval_jaxpr/gqhd,gkhd->ghqk/dot_general | solution.py:39
  151.3 12.6 %fusion.92 = (f32[8,4,64]{2,1,0:T(4,128)S(1)}, f32[8,4,64,1024]{3,2,1,0:T(8,128)}) fusion(f32[8,4,64,1024]{3,2,1,0:T(8,128)} %fusion.90, pred[8,64,1024]{2,1,0:T(8,128)(4,1)S(1)} %copy-done.1), kind=kOutput, calls=%fused_computation.100.clone.1 | output fusion | flops 12583935 | bytes 17309696 | tf_op jit(solution)/shard_map/while/body/eval_jaxpr/sub | solution.py:43
  163.9 5.4 fusion.93
  169.3 12.1 %multiply_convert_fusion.2 = bf16[8,4,64,1024]{3,2,1,0:T(8,128)(2,1)} fusion(f32[8,4,64]{2,1,0:T(4,128)S(1)} %fusion.93, f32[8,4,64,1024]{3,2,1,0:T(8,128)} %get-tuple-element.277, f32[8,4,64]{2,1,0:T(4,128)S(1)} %get-tuple-element.278, bf16[8,1024,4,128]{3,2,1,0:T(4,128)(2,1)} %reshape.484, bf16[8,64,4,128]{3,2,1,0:T(4,128)(2,1)S(1)} %reshape.485), kind=kOutput, calls=%fused_computation.12.clone.1 | convolution fusion | flops 545259520 | bytes 21512192 | tf_op jit(solution)/shard_map/while/body/eval_jaxpr/gqhd,gkhd->ghqk/dot_general | solution.py:48
  181.4 6.3 fusion.94
  192.8 11.5 %convolution_bitcast_fusion.2 = f32[8,1024,4,128]{1,3,2,0:T(8,128)} fusion(bf16[8,64,4,128]{3,2,1,0:T(4,128)(2,1)S(1)} %reshape.485, f32[8,4,64,1024]{3,2,1,0:T(8,128)} %get-tuple-element.277, f32[8,4,64]{2,1,0:T(4,128)S(1)} %get-tuple-element.278), kind=kOutput, calls=%fused_computation.11.clone.1 | convolution fusion | flops 541065216 | bytes 25698304 | tf_op jit(solution)/shard_map/while/body/eval_jaxpr/ghqk,gqhd->gkhd/dot_general | solution.py:59
  204.3 19.2 %copy.155 = f32[8,1024,4,128]{3,2,1,0:T(4,128)} copy(f32[8,1024,4,128]{1,3,2,0:T(8,128)} %convolution_bitcast_fusion.2) | data formatting | bytes 33554432 | tf_op jit(solution)/shard_map/while/body/eval_jaxpr/ghqk,gqhd->gkhd/transpose | solution.py:59
  223.5 19.9 %reshape.489 = f32[128,64,512]{2,1,0:T(8,128)} reshape(f32[8,1024,4,128]{3,2,1,0:T(4,128)} %copy.155) | data formatting | bytes 33554432 | tf_op jit(solution)/shard_map/while/body/eval_jaxpr/reshape | solution.py:63
  243.4 37.4 %scatter_fusion.1 = f32[32,64,512]{2,1,0:T(8,128)} fusion(f32[32,64,512]{2,1,0:T(8,128)} %get-tuple-element.293, s32[128]{0:T(128)S(1)} %fusion.89, f32[128,64,512]{2,1,0:T(8,128)} %reshape.489), kind=kCustom, calls=%fused_computation.6.clone.1 | custom fusion | flops 4194304 | bytes 50332160 | tf_op jit(solution)/shard_map/while/body/eval_jaxpr/scatter-add | solution.py:116
  280.9 10.3 %multiply_bitcast_fusion.2 = f32[8,1024,4,128]{1,3,2,0:T(8,128)} fusion(bf16[8,4,64,1024]{3,2,1,0:T(8,128)(2,1)} %multiply_convert_fusion.2, bf16[8,64,4,128]{3,2,1,0:T(4,128)(2,1)S(1)} %reshape.487), kind=kOutput, calls=%fused_computation.10.clone.1 | convolution fusion | flops 541065216 | bytes 21495808 | tf_op jit(solution)/shard_map/while/body/eval_jaxpr/ghqk,gqhd->gkhd/dot_general | solution.py:56
  291.1 19.2 %copy.154 = f32[8,1024,4,128]{3,2,1,0:T(4,128)} copy(f32[8,1024,4,128]{1,3,2,0:T(8,128)} %multiply_bitcast_fusion.2) | data formatting | bytes 33554432 | tf_op jit(solution)/shard_map/while/body/eval_jaxpr/mul | solution.py:56
  310.3 19.9 %reshape.488 = f32[128,64,512]{2,1,0:T(8,128)} reshape(f32[8,1024,4,128]{3,2,1,0:T(4,128)} %copy.154) | data formatting | bytes 33554432 | tf_op jit(solution)/shard_map/while/body/eval_jaxpr/reshape | solution.py:62
  330.3 37.2 %scatter_fusion = f32[32,64,512]{2,1,0:T(8,128)} fusion(f32[32,64,512]{2,1,0:T(8,128)} %get-tuple-element.292, s32[128]{0:T(128)S(1)} %fusion.89, f32[128,64,512]{2,1,0:T(8,128)} %reshape.488), kind=kCustom, calls=%fused_computation.5.clone.1 | custom fusion | flops 4194304 | bytes 50332160 | tf_op jit(solution)/shard_map/while/body/eval_jaxpr/scatter-add | solution.py:116
  367.8 2.8 gather_fusion.2
  376.7 6.5 gather_fusion.1
  383.2 12.5 %reshape.486 = bf16[8,1024,4,128]{3,2,1,0:T(4,128)(2,1)} reshape(bf16[128,64,512]{2,1,0:T(8,128)(2,1)} %gather_fusion.1) | data formatting | bytes 16777216 | tf_op jit(solution)/shard_map/while/body/eval_jaxpr/reshape;while/body/eval_jaxpr/reshape | solution.py:26
  395.7 8.1 %gather_fusion = bf16[128,64,512]{2,1,0:T(8,128)(2,1)} fusion(bf16[32,64,512]{2,1,0:T(8,128)(2,1)} %get-tuple-element.313, s32[1024]{0:T(1024)S(1)} %pad_clamp_fusion.3), kind=kCustom, calls=%fused_computation.2.clone.1 | custom fusion | bytes 16777728 | tf_op jit(solution)/shard_map/while/body/eval_jaxpr/gather | solution.py:113
  403.8 12.5 %reshape.484 = bf16[8,1024,4,128]{3,2,1,0:T(4,128)(2,1)} reshape(bf16[128,64,512]{2,1,0:T(8,128)(2,1)} %gather_fusion) | data formatting | bytes 16777216 | tf_op jit(solution)/shard_map/while/body/eval_jaxpr/reshape;while/body/eval_jaxpr/reshape | solution.py:27
  416.3 9.8 %fusion.90 = f32[8,4,64,1024]{3,2,1,0:T(8,128)} fusion(bf16[8,1024,4,128]{3,2,1,0:T(4,128)(2,1)} %reshape.486, bf16[8,64,4,128]{3,2,1,0:T(4,128)(2,1)S(1)} %reshape.487), kind=kOutput, calls=%fused_computation.21.clone.1 | convolution fusion | flops 536870912 | bytes 17301504 | tf_op jit(solution)/shard_map/while/body/eval_jaxpr/gqhd,gkhd->ghqk/dot_general | solution.py:39
  426.1 12.6 %fusion.92 = (f32[8,4,64]{2,1,0:T(4,128)S(1)}, f32[8,4,64,1024]{3,2,1,0:T(8,128)}) fusion(f32[8,4,64,1024]{3,2,1,0:T(8,128)} %fusion.90, pred[8,64,1024]{2,1,0:T(8,128)(4,1)S(1)} %copy-done.1), kind=kOutput, calls=%fused_computation.100.clone.1 | output fusion | flops 12583935 | bytes 17309696 | tf_op jit(solution)/shard_map/while/body/eval_jaxpr/sub | solution.py:43
  438.7 5.4 fusion.93
  444.1 12.1 %multiply_convert_fusion.2 = bf16[8,4,64,1024]{3,2,1,0:T(8,128)(2,1)} fusion(f32[8,4,64]{2,1,0:T(4,128)S(1)} %fusion.93, f32[8,4,64,1024]{3,2,1,0:T(8,128)} %get-tuple-element.277, f32[8,4,64]{2,1,0:T(4,128)S(1)} %get-tuple-element.278, bf16[8,1024,4,128]{3,2,1,0:T(4,128)(2,1)} %reshape.484, bf16[8,64,4,128]{3,2,1,0:T(4,128)(2,1)S(1)} %reshape.485), kind=kOutput, calls=%fused_computation.12.clone.1 | convolution fusion | flops 545259520 | bytes 21512192 | tf_op jit(solution)/shard_map/while/body/eval_jaxpr/gqhd,gkhd->ghqk/dot_general | solution.py:48
  456.2 6.3 fusion.94
  467.6 11.5 %convolution_bitcast_fusion.2 = f32[8,1024,4,128]{1,3,2,0:T(8,128)} fusion(bf16[8,64,4,128]{3,2,1,0:T(4,128)(2,1)S(1)} %reshape.485, f32[8,4,64,1024]{3,2,1,0:T(8,128)} %get-tuple-element.277, f32[8,4,64]{2,1,0:T(4,128)S(1)} %get-tuple-element.278), kind=kOutput, calls=%fused_computation.11.clone.1 | convolution fusion | flops 541065216 | bytes 25698304 | tf_op jit(solution)/shard_map/while/body/eval_jaxpr/ghqk,gqhd->gkhd/dot_general | solution.py:59
  479.1 19.2 %copy.155 = f32[8,1024,4,128]{3,2,1,0:T(4,128)} copy(f32[8,1024,4,128]{1,3,2,0:T(8,128)} %convolution_bitcast_fusion.2) | data formatting | bytes 33554432 | tf_op jit(solution)/shard_map/while/body/eval_jaxpr/ghqk,gqhd->gkhd/transpose | solution.py:59
  498.3 19.9 %reshape.489 = f32[128,64,512]{2,1,0:T(8,128)} reshape(f32[8,1024,4,128]{3,2,1,0:T(4,128)} %copy.155) | data formatting | bytes 33554432 | tf_op jit(solution)/shard_map/while/body/eval_jaxpr/reshape | solution.py:63
  518.2 38.1 %scatter_fusion.1 = f32[32,64,512]{2,1,0:T(8,128)} fusion(f32[32,64,512]{2,1,0:T(8,128)} %get-tuple-element.293, s32[128]{0:T(128)S(1)} %fusion.89, f32[128,64,512]{2,1,0:T(8,128)} %reshape.489), kind=kCustom, calls=%fused_computation.6.clone.1 | custom fusion | flops 4194304 | bytes 50332160 | tf_op jit(solution)/shard_map/while/body/eval_jaxpr/scatter-add | solution.py:116
  556.4 10.3 %multiply_bitcast_fusion.2 = f32[8,1024,4,128]{1,3,2,0:T(8,128)} fusion(bf16[8,4,64,1024]{3,2,1,0:T(8,128)(2,1)} %multiply_convert_fusion.2, bf16[8,64,4,128]{3,2,1,0:T(4,128)(2,1)S(1)} %reshape.487), kind=kOutput, calls=%fused_computation.10.clone.1 | convolution fusion | flops 541065216 | bytes 21495808 | tf_op jit(solution)/shard_map/while/body/eval_jaxpr/ghqk,gqhd->gkhd/dot_general | solution.py:56
  566.6 19.2 %copy.154 = f32[8,1024,4,128]{3,2,1,0:T(4,128)} copy(f32[8,1024,4,128]{1,3,2,0:T(8,128)} %multiply_bitcast_fusion.2) | data formatting | bytes 33554432 | tf_op jit(solution)/shard_map/while/body/eval_jaxpr/mul | solution.py:56
  585.8 19.9 %reshape.488 = f32[128,64,512]{2,1,0:T(8,128)} reshape(f32[8,1024,4,128]{3,2,1,0:T(4,128)} %copy.154) | data formatting | bytes 33554432 | tf_op jit(solution)/shard_map/while/body/eval_jaxpr/reshape | solution.py:62
  605.7 37.8 %scatter_fusion = f32[32,64,512]{2,1,0:T(8,128)} fusion(f32[32,64,512]{2,1,0:T(8,128)} %get-tuple-element.292, s32[128]{0:T(128)S(1)} %fusion.89, f32[128,64,512]{2,1,0:T(8,128)} %reshape.488), kind=kCustom, calls=%fused_computation.5.clone.1 | custom fusion | flops 4194304 | bytes 50332160 | tf_op jit(solution)/shard_map/while/body/eval_jaxpr/scatter-add | solution.py:116
  643.5 4.2 all-to-all-start.3
  647.7 5.0 slice_bitcast_fusion.1
  652.7 10.8 %all-to-all-done.3 = bf16[8,128,512]{2,1,0:T(8,128)(2,1)S(1)} async-done(((bf16[8,128,512]{2,1,0:T(8,128)(2,1)}), bf16[8,128,512]{2,1,0:T(8,128)(2,1)S(1)}, u32[]{:S(2)}, u32[]{:S(2)}) %all-to-all-start.3) | async-done | bytes 1048608 | tf_op jit(solution)/shard_map/all_to_all | solution.py:145
  663.5 10.3 %all-to-all-start.4 = ((f32[16,1,64,512]{3,2,1,0:T(8,128)}), f32[16,1,64,512]{3,2,1,0:T(8,128)}, u32[]{:S(2)}, u32[]{:S(2)}) async-start(f32[16,1,64,512]{3,2,1,0:T(8,128)} %get-tuple-element.188), calls=%async_computation.4 | async-start | bytes 4194304 | tf_op jit(solution)/shard_map/all_to_all | solution.py:122
  673.8 4.2 slice_bitcast_fusion
  678.0 24.4 %all-to-all-done.4 = f32[16,1,64,512]{3,2,1,0:T(8,128)} async-done(((f32[16,1,64,512]{3,2,1,0:T(8,128)}), f32[16,1,64,512]{3,2,1,0:T(8,128)}, u32[]{:S(2)}, u32[]{:S(2)}) %all-to-all-start.4) | async-done | bytes 2097184 | tf_op jit(solution)/shard_map/all_to_all | solution.py:122
  702.4 7.1 all-to-all-start.6
  709.6 5.1 scatter_fusion.2
  714.6 2.7 convert_element_type.40
  717.3 20.8 %all-to-all-done.6 = f32[16,1,64,512]{3,2,1,0:T(8,128)} async-done(((f32[16,1,64,512]{3,2,1,0:T(8,128)}), f32[16,1,64,512]{3,2,1,0:T(8,128)}, u32[]{:S(2)}, u32[]{:S(2)}) %all-to-all-start.6) | async-done | bytes 2097184 | tf_op jit(solution)/shard_map/all_to_all | solution.py:129
  738.1 4.2 all-to-all-start.5
  742.4 3.5 scatter_fusion.3
  747.1 11.1 %all-to-all-done.5 = bf16[8,128,512]{2,1,0:T(8,128)(2,1)} async-done(((bf16[8,128,512]{2,1,0:T(8,128)(2,1)}), bf16[8,128,512]{2,1,0:T(8,128)(2,1)}, u32[]{:S(2)}, u32[]{:S(2)}) %all-to-all-start.5) | async-done | bytes 1048608 | tf_op jit(solution)/shard_map/all_to_all | solution.py:146
  758.2 3.6 all-to-all-start.7
  766.7 10.9 %all-to-all-done.7 = bf16[8,128,512]{2,1,0:T(8,128)(2,1)S(1)} async-done(((bf16[8,128,512]{2,1,0:T(8,128)(2,1)}), bf16[8,128,512]{2,1,0:T(8,128)(2,1)S(1)}, u32[]{:S(2)}, u32[]{:S(2)}) %all-to-all-start.7) | async-done | bytes 1048608 | tf_op jit(solution)/shard_map/all_to_all | solution.py:147
  (93 shorter events, 34.6 us)
Async XLA Ops:
  0.6 55.1 %copy-start.4 = (s32[16,16]{1,0:T(8,128)S(1)}, s32[16,16]{1,0:T(8,128)}, u32[]{:S(2)}) copy-start(s32[16,16]{1,0:T(8,128)} %param.11) | copy-start | bytes 3076
  0.6 55.1 %copy-start.2 = (bf16[1024,512]{1,0:T(8,128)(2,1)S(1)}, bf16[1024,512]{1,0:T(8,128)(2,1)}, u32[]{:S(2)}) copy-start(bf16[1024,512]{1,0:T(8,128)(2,1)} %param.8) | copy-start | bytes 3145732
  24.0 21.4 %all-to-all-start.1 = ((bf16[16,1,64,512]{3,2,1,0:T(8,128)(2,1)}), bf16[16,1,64,512]{3,2,1,0:T(8,128)(2,1)S(1)}, u32[]{:S(2)}, u32[]{:S(2)}) async-start(bf16[16,1,64,512]{3,2,1,0:T(8,128)(2,1)} %bitcast.19), calls=%async_computation.1 | async-start | bytes 2097152 | tf_op jit(solution)/shard_map/all_to_all | solution.py:90
  45.4 10.4 %copy-start.3 = (bf16[16,1,64,512]{3,2,1,0:T(8,128)(2,1)}, bf16[16,1,64,512]{3,2,1,0:T(8,128)(2,1)S(1)}, u32[]{:S(2)}) copy-start(bf16[16,1,64,512]{3,2,1,0:T(8,128)(2,1)S(1)} %all-to-all-done.1) | copy-start | bytes 3145732
  45.4 22.4 %all-to-all-start.2 = ((bf16[16,1,64,512]{3,2,1,0:T(8,128)(2,1)}), bf16[16,1,64,512]{3,2,1,0:T(8,128)(2,1)}, u32[]{:S(2)}, u32[]{:S(2)}) async-start(bf16[16,1,64,512]{3,2,1,0:T(8,128)(2,1)} %bitcast.23), calls=%async_computation.2 | async-start | bytes 2097152 | tf_op jit(solution)/shard_map/all_to_all | solution.py:91
  141.5 9.8 %copy-start.1 = (pred[8,64,1024]{2,1,0:T(8,128)(4,1)S(1)}, pred[8,64,1024]{2,1,0:T(8,128)(4,1)}, u32[]{:S(2)}) copy-start(pred[8,64,1024]{2,1,0:T(8,128)(4,1)} %or_and_fusion.2) | copy-start | bytes 1572868 | tf_op jit(solution)/shard_map/while
  141.5 22.3 %slice-start = ((s8[8388608]{0:T(1024)(128)(4,1)}), s8[4194304]{0:T(1024)(128)(4,1)S(1)}, s32[]{:S(2)}) async-start(s8[8388608]{0:T(1024)(128)(4,1)} %bitcast.97), calls=%async_computation.8 | async-start | bytes 8388608 | tf_op jit(solution)/shard_map/while
  151.3 12.6 %slice-start.1 = ((s8[8388608]{0:T(1024)(128)(4,1)}), s8[4194304]{0:T(1024)(128)(4,1)S(1)}, s32[]{:S(2)}) async-start(s8[8388608]{0:T(1024)(128)(4,1)} %bitcast.97), calls=%async_computation.9 | async-start | bytes 8388608 | tf_op jit(solution)/shard_map/while
  151.3 12.6 %copy-start = (f32[8,4,64,128]{3,1,2,0:T(4,128)S(1)}, f32[8,4,64,128]{3,1,2,0:T(4,128)}, u32[]{:S(2)}) copy-start(f32[8,4,64,128]{3,1,2,0:T(4,128)} %bitcast_convert_fusion.2) | copy-start | bytes 3145732 | tf_op jit(solution)/shard_map/while
  416.3 9.8 %copy-start.1 = (pred[8,64,1024]{2,1,0:T(8,128)(4,1)S(1)}, pred[8,64,1024]{2,1,0:T(8,128)(4,1)}, u32[]{:S(2)}) copy-start(pred[8,64,1024]{2,1,0:T(8,128)(4,1)} %or_and_fusion.2) | copy-start | bytes 1572868 | tf_op jit(solution)/shard_map/while
  416.3 22.3 %slice-start = ((s8[8388608]{0:T(1024)(128)(4,1)}), s8[4194304]{0:T(1024)(128)(4,1)S(1)}, s32[]{:S(2)}) async-start(s8[8388608]{0:T(1024)(128)(4,1)} %bitcast.97), calls=%async_computation.8 | async-start | bytes 8388608 | tf_op jit(solution)/shard_map/while
  426.1 12.6 %slice-start.1 = ((s8[8388608]{0:T(1024)(128)(4,1)}), s8[4194304]{0:T(1024)(128)(4,1)S(1)}, s32[]{:S(2)}) async-start(s8[8388608]{0:T(1024)(128)(4,1)} %bitcast.97), calls=%async_computation.9 | async-start | bytes 8388608 | tf_op jit(solution)/shard_map/while
  426.1 12.6 %copy-start = (f32[8,4,64,128]{3,1,2,0:T(4,128)S(1)}, f32[8,4,64,128]{3,1,2,0:T(4,128)}, u32[]{:S(2)}) copy-start(f32[8,4,64,128]{3,1,2,0:T(4,128)} %bitcast_convert_fusion.2) | copy-start | bytes 3145732 | tf_op jit(solution)/shard_map/while
  643.5 20.0 %all-to-all-start.3 = ((bf16[8,128,512]{2,1,0:T(8,128)(2,1)}), bf16[8,128,512]{2,1,0:T(8,128)(2,1)S(1)}, u32[]{:S(2)}, u32[]{:S(2)}) async-start(bf16[8,128,512]{2,1,0:T(8,128)(2,1)} %bitcast.109), calls=%async_computation.3 | async-start | bytes 2097152 | tf_op jit(solution)/shard_map/all_to_all | solution.py:145
  663.5 46.0 %copy-start.5 = (s32[16]{0:T(128)S(1)}, s32[16]{0:T(128)}, u32[]{:S(2)}) copy-start(s32[16]{0:T(128)} %get-tuple-element.154) | copy-start | bytes 196
  663.5 38.9 %all-to-all-start.4 = ((f32[16,1,64,512]{3,2,1,0:T(8,128)}), f32[16,1,64,512]{3,2,1,0:T(8,128)}, u32[]{:S(2)}, u32[]{:S(2)}) async-start(f32[16,1,64,512]{3,2,1,0:T(8,128)} %get-tuple-element.188), calls=%async_computation.4 | async-start | bytes 4194304 | tf_op jit(solution)/shard_map/all_to_all | solution.py:122
  702.4 35.7 %all-to-all-start.6 = ((f32[16,1,64,512]{3,2,1,0:T(8,128)}), f32[16,1,64,512]{3,2,1,0:T(8,128)}, u32[]{:S(2)}, u32[]{:S(2)}) async-start(f32[16,1,64,512]{3,2,1,0:T(8,128)} %get-tuple-element.186), calls=%async_computation.6 | async-start | bytes 4194304 | tf_op jit(solution)/shard_map/all_to_all | solution.py:129
  738.1 20.1 %all-to-all-start.5 = ((bf16[8,128,512]{2,1,0:T(8,128)(2,1)}), bf16[8,128,512]{2,1,0:T(8,128)(2,1)}, u32[]{:S(2)}, u32[]{:S(2)}) async-start(bf16[8,128,512]{2,1,0:T(8,128)(2,1)} %bitcast.31), calls=%async_computation.5 | async-start | bytes 2097152 | tf_op jit(solution)/shard_map/all_to_all | solution.py:146
  758.2 19.3 %all-to-all-start.7 = ((bf16[8,128,512]{2,1,0:T(8,128)(2,1)}), bf16[8,128,512]{2,1,0:T(8,128)(2,1)S(1)}, u32[]{:S(2)}, u32[]{:S(2)}) async-start(bf16[8,128,512]{2,1,0:T(8,128)(2,1)} %bitcast.36), calls=%async_computation.7 | async-start | bytes 2097152 | tf_op jit(solution)/shard_map/all_to_all | solution.py:147
where the time goes:
time: 790 us; the launch traced here: 780 us
  local copies, waits for them, and re-layouts  286 us (36%)
  other arithmetic  207 us (26%)
  matrix products  111 us (14%)
  waiting for transfers between devices  103 us (13%)
  starting transfers between devices  38.5 us (5%)
  loops' own time  17.4 us (2%)
  blocking collectives  16.2 us (2%)
    scatter-add x2, other arithmetic, advance(): grad_values.at[flat].add(dvalue)  75.6 us
    scatter-add x2, other arithmetic, advance(): grad_keys.at[flat].add(dkey)  74.9 us
    reshape x2, local copies, waits for them, and re-layouts, group_grads(): dvalue.reshape(count * TOPK, BLOCK, width)  39.8 us
    reshape x2, local copies, waits for them, and re-layouts, group_grads(): dkey.reshape(count * TOPK, BLOCK, width)  39.8 us
    transpose x2, local copies, waits for them, and re-layouts, group_grads(): jnp.einsum('ghqk,gqhd->gkhd', probs_low, grad_h, preferred_element_type=j...  38.4 us
    mul x2, local copies, waits for them, and re-layouts, group_grads(): jnp.einsum('ghqk,gqhd->gkhd', dscores_low, query_h, preferred_element_typ...  38.4 us
    sub x2, other arithmetic, group_grads(): expo = jnp.exp(scores - highest)  25.1 us
    reshape x2, local copies, waits for them, and re-layouts, group_grads(): key_h = key_blk.reshape(count, TOPK * BLOCK, HEAD_DEV, HDIM)  25.1 us
  transfers between devices with their start and end apart: 7, of which 7 were waited for; matrix products, arithmetic and copies ran while one was open for 5% of the time, Pallas kernels for 0%

commit v1 on v0

--- a/solution.py
+++ b/solution.py
@@ -143,7 +143,12 @@
     value_local = value_total.reshape(per_dev * BLOCK, width).astype(jnp.bfloat16)
     query_out, key_out, value_out = (
         lax.all_to_all(query_local, "head", split_axis=0, concat_axis=1, tiled=True),
-        lax.all_to_all(key_local, "head", split_axis=0, concat_axis=1, tiled=True),
+        jnp.concatenate(
+            lax.all_to_all(
+                jnp.stack(jnp.split(key_local, lax.axis_size("head"), axis=0)), "head", 0, 0
+            ),
+            axis=1,
+        ),
         lax.all_to_all(value_local, "head", split_axis=0, concat_axis=1, tiled=True),
     )
     return (query_out, key_out, value_out)

time: 790 us -> 790 us (level)
  no operation moved by 1% of the time
where the time goes in v1:
time: 790 us; the launch traced here: 780 us
  local copies, waits for them, and re-layouts  291 us (37%)
  other arithmetic  206 us (26%)
  matrix products  111 us (14%)
  waiting for transfers between devices  98.6 us (12%)
  starting transfers between devices  38.5 us (5%)
  loops' own time  17.4 us (2%)
  blocking collectives  16.2 us (2%)
    scatter-add x2, other arithmetic, advance(): grad_values.at[flat].add(dvalue)  75.6 us
    scatter-add x2, other arithmetic, advance(): grad_keys.at[flat].add(dkey)  74.9 us
    reshape x2, local copies, waits for them, and re-layouts, group_grads(): dvalue.reshape(count * TOPK, BLOCK, width)  39.8 us
    reshape x2, local copies, waits for them, and re-layouts, group_grads(): dkey.reshape(count * TOPK, BLOCK, width)  39.8 us
    transpose x2, local copies, waits for them, and re-layouts, group_grads(): jnp.einsum('ghqk,gqhd->gkhd', probs_low, grad_h, preferred_element_type=j...  38.4 us
    mul x2, local copies, waits for them, and re-layouts, group_grads(): jnp.einsum('ghqk,gqhd->gkhd', dscores_low, query_h, preferred_element_typ...  38.4 us
    sub x2, other arithmetic, group_grads(): expo = jnp.exp(scores - highest)  25.1 us
    reshape x2, local copies, waits for them, and re-layouts, group_grads(): key_h = key_blk.reshape(count, TOPK * BLOCK, HEAD_DEV, HDIM)  25.1 us
  transfers between devices with their start and end apart: 7, of which 7 were waited for; matrix products, arithmetic and copies ran while one was open for 5% of the time, Pallas kernels for 0%

profile of v1, /device:TPU:1, one launch (start us, length us, event | category | flops | bytes accessed | tf_op | source)
XLA Modules:
  0.0 779.9 jit_solution(1943042083959756693)
XLA Ops:
  3.8 16.2 %all_to_all.72 = s32[16,1,1]{2,1,0:T(1,128)S(1)} all-to-all(s32[16,1,1]{2,1,0:T(1,128)S(1)} %copy.97), channel_id=1, replica_groups=mesh['ctx'=16,'head'=8] {'ctx'}, dimensions={0} | all-to-all | bytes 128 | tf_op jit(solution)/shard_map/all_to_all | solution.py:84
  21.2 2.8 gather_fusion.3
  24.0 4.1 all-to-all-start.1
  28.1 2.8 gather_fusion.4
  30.9 14.5 %all-to-all-done.1 = bf16[16,1,64,512]{3,2,1,0:T(8,128)(2,1)S(1)} async-done(((bf16[16,1,64,512]{3,2,1,0:T(8,128)(2,1)}), bf16[16,1,64,512]{3,2,1,0:T(8,128)(2,1)S(1)}, u32[]{:S(2)}, u32[]{:S(2)}) %all-to-all-start.1) | async-done | bytes 1048608 | tf_op jit(solution)/shard_map/all_to_all | solution.py:90
  45.4 5.0 all-to-all-start.2
  50.4 5.4 fusion.47
  57.2 10.6 %all-to-all-done.2 = bf16[16,1,64,512]{3,2,1,0:T(8,128)(2,1)} async-done(((bf16[16,1,64,512]{3,2,1,0:T(8,128)(2,1)}), bf16[16,1,64,512]{3,2,1,0:T(8,128)(2,1)}, u32[]{:S(2)}, u32[]{:S(2)}) %all-to-all-start.2) | async-done | bytes 1048608 | tf_op jit(solution)/shard_map/all_to_all | solution.py:91
  67.8 3.1 pad_maximum_fusion.1
  70.8 2.4 broadcast_in_dim.72.clone
  73.3 2.5 broadcast_in_dim.72
  75.8 567.8 %while.16 = (s32[]{:T(128)}, f32[32,64,512]{2,1,0:T(8,128)}, f32[32,64,512]{2,1,0:T(8,128)}, bf16[2,8,64,512]{3,2,1,0:T(8,128)(2,1)}, s32[2,8,16]{2,1,0:T(8,128)...) while((s32[]{:T(128)}, f32[32,64,512]{2,1,0:T(8,128)}, ...), condition=%wide.region_9.10_spmd, body=%wide.region_4.9_spmd.sunk | while | flops 3265628928 | bytes 477484352 | solution.py:119
  93.3 2.8 gather_fusion.2
  97.7 2.1 constant_dynamic-slice_fusion.6
  102.2 6.3 gather_fusion.1
  108.5 12.5 %reshape.506 = bf16[8,1024,4,128]{3,2,1,0:T(4,128)(2,1)} reshape(bf16[128,64,512]{2,1,0:T(8,128)(2,1)} %gather_fusion.1) | data formatting | bytes 16777216 | tf_op jit(solution)/shard_map/while/body/eval_jaxpr/reshape;while/body/eval_jaxpr/reshape | solution.py:26
  121.0 7.9 %gather_fusion = bf16[128,64,512]{2,1,0:T(8,128)(2,1)} fusion(bf16[32,64,512]{2,1,0:T(8,128)(2,1)} %get-tuple-element.321, s32[1024]{0:T(1024)S(1)} %pad_clamp_fusion.3), kind=kCustom, calls=%fused_computation.2.clone.1 | custom fusion | bytes 16777728 | tf_op jit(solution)/shard_map/while/body/eval_jaxpr/gather | solution.py:113
  129.0 12.5 %reshape.504 = bf16[8,1024,4,128]{3,2,1,0:T(4,128)(2,1)} reshape(bf16[128,64,512]{2,1,0:T(8,128)(2,1)} %gather_fusion) | data formatting | bytes 16777216 | tf_op jit(solution)/shard_map/while/body/eval_jaxpr/reshape;while/body/eval_jaxpr/reshape | solution.py:27
  141.5 9.8 %fusion.91 = f32[8,4,64,1024]{3,2,1,0:T(8,128)} fusion(bf16[8,1024,4,128]{3,2,1,0:T(4,128)(2,1)} %reshape.506, bf16[8,64,4,128]{3,2,1,0:T(4,128)(2,1)S(1)} %reshape.507), kind=kOutput, calls=%fused_computation.21.clone.1 | convolution fusion | flops 536870912 | bytes 17301504 | tf_op jit(solution)/shard_map/while/body/eval_jaxpr/gqhd,gkhd->ghqk/dot_general | solution.py:39
  151.3 12.6 %fusion.93 = (f32[8,4,64]{2,1,0:T(4,128)S(1)}, f32[8,4,64,1024]{3,2,1,0:T(8,128)}) fusion(f32[8,4,64,1024]{3,2,1,0:T(8,128)} %fusion.91, pred[8,64,1024]{2,1,0:T(8,128)(4,1)S(1)} %copy-done.1), kind=kOutput, calls=%fused_computation.108.clone.1 | output fusion | flops 12583935 | bytes 17309696 | tf_op jit(solution)/shard_map/while/body/eval_jaxpr/sub | solution.py:43
  163.9 5.4 fusion.94
  169.3 12.1 %multiply_convert_fusion.2 = bf16[8,4,64,1024]{3,2,1,0:T(8,128)(2,1)} fusion(f32[8,4,64]{2,1,0:T(4,128)S(1)} %fusion.94, f32[8,4,64,1024]{3,2,1,0:T(8,128)} %get-tuple-element.285, f32[8,4,64]{2,1,0:T(4,128)S(1)} %get-tuple-element.286, bf16[8,1024,4,128]{3,2,1,0:T(4,128)(2,1)} %reshape.504, bf16[8,64,4,128]{3,2,1,0:T(4,128)(2,1)S(1)} %reshape.505), kind=kOutput, calls=%fused_computation.12.clone.1 | convolution fusion | flops 545259520 | bytes 21512192 | tf_op jit(solution)/shard_map/while/body/eval_jaxpr/gqhd,gkhd->ghqk/dot_general | solution.py:48
  181.4 6.3 fusion.95
  192.8 11.5 %convolution_bitcast_fusion.2 = f32[8,1024,4,128]{1,3,2,0:T(8,128)} fusion(bf16[8,64,4,128]{3,2,1,0:T(4,128)(2,1)S(1)} %reshape.505, f32[8,4,64,1024]{3,2,1,0:T(8,128)} %get-tuple-element.285, f32[8,4,64]{2,1,0:T(4,128)S(1)} %get-tuple-element.286), kind=kOutput, calls=%fused_computation.11.clone.1 | convolution fusion | flops 541065216 | bytes 25698304 | tf_op jit(solution)/shard_map/while/body/eval_jaxpr/ghqk,gqhd->gkhd/dot_general | solution.py:59
  204.3 19.2 %copy.169 = f32[8,1024,4,128]{3,2,1,0:T(4,128)} copy(f32[8,1024,4,128]{1,3,2,0:T(8,128)} %convolution_bitcast_fusion.2) | data formatting | bytes 33554432 | tf_op jit(solution)/shard_map/while/body/eval_jaxpr/ghqk,gqhd->gkhd/transpose | solution.py:59
  223.5 19.9 %reshape.509 = f32[128,64,512]{2,1,0:T(8,128)} reshape(f32[8,1024,4,128]{3,2,1,0:T(4,128)} %copy.169) | data formatting | bytes 33554432 | tf_op jit(solution)/shard_map/while/body/eval_jaxpr/reshape | solution.py:63
  243.4 37.4 %scatter_fusion.1 = f32[32,64,512]{2,1,0:T(8,128)} fusion(f32[32,64,512]{2,1,0:T(8,128)} %get-tuple-element.301, s32[128]{0:T(128)S(1)} %fusion.90, f32[128,64,512]{2,1,0:T(8,128)} %reshape.509), kind=kCustom, calls=%fused_computation.6.clone.1 | custom fusion | flops 4194304 | bytes 50332160 | tf_op jit(solution)/shard_map/while/body/eval_jaxpr/scatter-add | solution.py:116
  280.9 10.3 %multiply_bitcast_fusion.2 = f32[8,1024,4,128]{1,3,2,0:T(8,128)} fusion(bf16[8,4,64,1024]{3,2,1,0:T(8,128)(2,1)} %multiply_convert_fusion.2, bf16[8,64,4,128]{3,2,1,0:T(4,128)(2,1)S(1)} %reshape.507), kind=kOutput, calls=%fused_computation.10.clone.1 | convolution fusion | flops 541065216 | bytes 21495808 | tf_op jit(solution)/shard_map/while/body/eval_jaxpr/ghqk,gqhd->gkhd/dot_general | solution.py:56
  291.1 19.2 %copy.168 = f32[8,1024,4,128]{3,2,1,0:T(4,128)} copy(f32[8,1024,4,128]{1,3,2,0:T(8,128)} %multiply_bitcast_fusion.2) | data formatting | bytes 33554432 | tf_op jit(solution)/shard_map/while/body/eval_jaxpr/mul | solution.py:56
  310.3 19.9 %reshape.508 = f32[128,64,512]{2,1,0:T(8,128)} reshape(f32[8,1024,4,128]{3,2,1,0:T(4,128)} %copy.168) | data formatting | bytes 33554432 | tf_op jit(solution)/shard_map/while/body/eval_jaxpr/reshape | solution.py:62
  330.3 37.2 %scatter_fusion = f32[32,64,512]{2,1,0:T(8,128)} fusion(f32[32,64,512]{2,1,0:T(8,128)} %get-tuple-element.300, s32[128]{0:T(128)S(1)} %fusion.90, f32[128,64,512]{2,1,0:T(8,128)} %reshape.508), kind=kCustom, calls=%fused_computation.5.clone.1 | custom fusion | flops 4194304 | bytes 50332160 | tf_op jit(solution)/shard_map/while/body/eval_jaxpr/scatter-add | solution.py:116
  367.8 2.8 gather_fusion.2
  372.2 2.1 constant_dynamic-slice_fusion.6
  376.7 6.5 gather_fusion.1
  383.2 12.5 %reshape.506 = bf16[8,1024,4,128]{3,2,1,0:T(4,128)(2,1)} reshape(bf16[128,64,512]{2,1,0:T(8,128)(2,1)} %gather_fusion.1) | data formatting | bytes 16777216 | tf_op jit(solution)/shard_map/while/body/eval_jaxpr/reshape;while/body/eval_jaxpr/reshape | solution.py:26
  395.7 8.1 %gather_fusion = bf16[128,64,512]{2,1,0:T(8,128)(2,1)} fusion(bf16[32,64,512]{2,1,0:T(8,128)(2,1)} %get-tuple-element.321, s32[1024]{0:T(1024)S(1)} %pad_clamp_fusion.3), kind=kCustom, calls=%fused_computation.2.clone.1 | custom fusion | bytes 16777728 | tf_op jit(solution)/shard_map/while/body/eval_jaxpr/gather | solution.py:113
  403.8 12.5 %reshape.504 = bf16[8,1024,4,128]{3,2,1,0:T(4,128)(2,1)} reshape(bf16[128,64,512]{2,1,0:T(8,128)(2,1)} %gather_fusion) | data formatting | bytes 16777216 | tf_op jit(solution)/shard_map/while/body/eval_jaxpr/reshape;while/body/eval_jaxpr/reshape | solution.py:27
  416.3 9.8 %fusion.91 = f32[8,4,64,1024]{3,2,1,0:T(8,128)} fusion(bf16[8,1024,4,128]{3,2,1,0:T(4,128)(2,1)} %reshape.506, bf16[8,64,4,128]{3,2,1,0:T(4,128)(2,1)S(1)} %reshape.507), kind=kOutput, calls=%fused_computation.21.clone.1 | convolution fusion | flops 536870912 | bytes 17301504 | tf_op jit(solution)/shard_map/while/body/eval_jaxpr/gqhd,gkhd->ghqk/dot_general | solution.py:39
  426.1 12.6 %fusion.93 = (f32[8,4,64]{2,1,0:T(4,128)S(1)}, f32[8,4,64,1024]{3,2,1,0:T(8,128)}) fusion(f32[8,4,64,1024]{3,2,1,0:T(8,128)} %fusion.91, pred[8,64,1024]{2,1,0:T(8,128)(4,1)S(1)} %copy-done.1), kind=kOutput, calls=%fused_computation.108.clone.1 | output fusion | flops 12583935 | bytes 17309696 | tf_op jit(solution)/shard_map/while/body/eval_jaxpr/sub | solution.py:43
  438.7 5.4 fusion.94
  444.1 12.1 %multiply_convert_fusion.2 = bf16[8,4,64,1024]{3,2,1,0:T(8,128)(2,1)} fusion(f32[8,4,64]{2,1,0:T(4,128)S(1)} %fusion.94, f32[8,4,64,1024]{3,2,1,0:T(8,128)} %get-tuple-element.285, f32[8,4,64]{2,1,0:T(4,128)S(1)} %get-tuple-element.286, bf16[8,1024,4,128]{3,2,1,0:T(4,128)(2,1)} %reshape.504, bf16[8,64,4,128]{3,2,1,0:T(4,128)(2,1)S(1)} %reshape.505), kind=kOutput, calls=%fused_computation.12.clone.1 | convolution fusion | flops 545259520 | bytes 21512192 | tf_op jit(solution)/shard_map/while/body/eval_jaxpr/gqhd,gkhd->ghqk/dot_general | solution.py:48
  456.2 6.3 fusion.95
  467.6 11.5 %convolution_bitcast_fusion.2 = f32[8,1024,4,128]{1,3,2,0:T(8,128)} fusion(bf16[8,64,4,128]{3,2,1,0:T(4,128)(2,1)S(1)} %reshape.505, f32[8,4,64,1024]{3,2,1,0:T(8,128)} %get-tuple-element.285, f32[8,4,64]{2,1,0:T(4,128)S(1)} %get-tuple-element.286), kind=kOutput, calls=%fused_computation.11.clone.1 | convolution fusion | flops 541065216 | bytes 25698304 | tf_op jit(solution)/shard_map/while/body/eval_jaxpr/ghqk,gqhd->gkhd/dot_general | solution.py:59
  479.1 19.2 %copy.169 = f32[8,1024,4,128]{3,2,1,0:T(4,128)} copy(f32[8,1024,4,128]{1,3,2,0:T(8,128)} %convolution_bitcast_fusion.2) | data formatting | bytes 33554432 | tf_op jit(solution)/shard_map/while/body/eval_jaxpr/ghqk,gqhd->gkhd/transpose | solution.py:59
  498.3 19.9 %reshape.509 = f32[128,64,512]{2,1,0:T(8,128)} reshape(f32[8,1024,4,128]{3,2,1,0:T(4,128)} %copy.169) | data formatting | bytes 33554432 | tf_op jit(solution)/shard_map/while/body/eval_jaxpr/reshape | solution.py:63
  518.2 38.1 %scatter_fusion.1 = f32[32,64,512]{2,1,0:T(8,128)} fusion(f32[32,64,512]{2,1,0:T(8,128)} %get-tuple-element.301, s32[128]{0:T(128)S(1)} %fusion.90, f32[128,64,512]{2,1,0:T(8,128)} %reshape.509), kind=kCustom, calls=%fused_computation.6.clone.1 | custom fusion | flops 4194304 | bytes 50332160 | tf_op jit(solution)/shard_map/while/body/eval_jaxpr/scatter-add | solution.py:116
  556.4 10.3 %multiply_bitcast_fusion.2 = f32[8,1024,4,128]{1,3,2,0:T(8,128)} fusion(bf16[8,4,64,1024]{3,2,1,0:T(8,128)(2,1)} %multiply_convert_fusion.2, bf16[8,64,4,128]{3,2,1,0:T(4,128)(2,1)S(1)} %reshape.507), kind=kOutput, calls=%fused_computation.10.clone.1 | convolution fusion | flops 541065216 | bytes 21495808 | tf_op jit(solution)/shard_map/while/body/eval_jaxpr/ghqk,gqhd->gkhd/dot_general | solution.py:56
  566.6 19.2 %copy.168 = f32[8,1024,4,128]{3,2,1,0:T(4,128)} copy(f32[8,1024,4,128]{1,3,2,0:T(8,128)} %multiply_bitcast_fusion.2) | data formatting | bytes 33554432 | tf_op jit(solution)/shard_map/while/body/eval_jaxpr/mul | solution.py:56
  585.8 19.9 %reshape.508 = f32[128,64,512]{2,1,0:T(8,128)} reshape(f32[8,1024,4,128]{3,2,1,0:T(4,128)} %copy.168) | data formatting | bytes 33554432 | tf_op jit(solution)/shard_map/while/body/eval_jaxpr/reshape | solution.py:62
  605.7 37.8 %scatter_fusion = f32[32,64,512]{2,1,0:T(8,128)} fusion(f32[32,64,512]{2,1,0:T(8,128)} %get-tuple-element.300, s32[128]{0:T(128)S(1)} %fusion.90, f32[128,64,512]{2,1,0:T(8,128)} %reshape.508), kind=kCustom, calls=%fused_computation.5.clone.1 | custom fusion | flops 4194304 | bytes 50332160 | tf_op jit(solution)/shard_map/while/body/eval_jaxpr/scatter-add | solution.py:116
  643.5 4.2 all-to-all-start.3
  647.7 5.0 slice_bitcast_fusion.1
  652.7 10.8 %all-to-all-done.3 = bf16[8,128,512]{2,1,0:T(8,128)(2,1)S(1)} async-done(((bf16[8,128,512]{2,1,0:T(8,128)(2,1)}), bf16[8,128,512]{2,1,0:T(8,128)(2,1)S(1)}, u32[]{:S(2)}, u32[]{:S(2)}) %all-to-all-start.3) | async-done | bytes 1048608 | tf_op jit(solution)/shard_map/all_to_all | solution.py:145
  663.5 10.3 %all-to-all-start.4 = ((f32[16,1,64,512]{3,2,1,0:T(8,128)}), f32[16,1,64,512]{3,2,1,0:T(8,128)}, u32[]{:S(2)}, u32[]{:S(2)}) async-start(f32[16,1,64,512]{3,2,1,0:T(8,128)} %get-tuple-element.188), calls=%async_computation.4 | async-start | bytes 4194304 | tf_op jit(solution)/shard_map/all_to_all | solution.py:122
  673.8 4.2 slice_bitcast_fusion
  678.0 24.4 %all-to-all-done.4 = f32[16,1,64,512]{3,2,1,0:T(8,128)} async-done(((f32[16,1,64,512]{3,2,1,0:T(8,128)}), f32[16,1,64,512]{3,2,1,0:T(8,128)}, u32[]{:S(2)}, u32[]{:S(2)}) %all-to-all-start.4) | async-done | bytes 2097184 | tf_op jit(solution)/shard_map/all_to_all | solution.py:122
  702.4 7.1 all-to-all-start.6
  709.6 5.1 scatter_fusion.2
  721.8 16.4 %all-to-all-done.6 = f32[16,1,64,512]{3,2,1,0:T(8,128)} async-done(((f32[16,1,64,512]{3,2,1,0:T(8,128)}), f32[16,1,64,512]{3,2,1,0:T(8,128)}, u32[]{:S(2)}, u32[]{:S(2)}) %all-to-all-start.6) | async-done | bytes 2097184 | tf_op jit(solution)/shard_map/all_to_all | solution.py:129
  738.1 4.2 all-to-all-start.5
  742.4 3.5 scatter_fusion.3
  747.1 11.1 %all-to-all-done.5 = bf16[8,128,512]{2,1,0:T(8,128)(2,1)} async-done(((bf16[8,128,512]{2,1,0:T(8,128)(2,1)}), bf16[8,128,512]{2,1,0:T(8,128)(2,1)}, u32[]{:S(2)}, u32[]{:S(2)}) %all-to-all-start.5) | async-done | bytes 1048608 | tf_op jit(solution)/shard_map/all_to_all | solution.py:147
  758.2 3.6 all-to-all-start.7
  766.7 10.9 %all-to-all-done.7 = bf16[8,128,512]{2,1,0:T(8,128)(2,1)S(1)} async-done(((bf16[8,128,512]{2,1,0:T(8,128)(2,1)}), bf16[8,128,512]{2,1,0:T(8,128)(2,1)S(1)}, u32[]{:S(2)}, u32[]{:S(2)}) %all-to-all-start.7) | async-done | bytes 1048608 | tf_op jit(solution)/shard_map/all_to_all | solution.py:152
  (102 shorter events, 39.7 us)
Async XLA Ops:
  0.6 55.1 %copy-start.4 = (s32[16,16]{1,0:T(8,128)S(1)}, s32[16,16]{1,0:T(8,128)}, u32[]{:S(2)}) copy-start(s32[16,16]{1,0:T(8,128)} %param.11) | copy-start | bytes 3076
  0.6 55.1 %copy-start.2 = (bf16[1024,512]{1,0:T(8,128)(2,1)S(1)}, bf16[1024,512]{1,0:T(8,128)(2,1)}, u32[]{:S(2)}) copy-start(bf16[1024,512]{1,0:T(8,128)(2,1)} %param.8) | copy-start | bytes 3145732
  24.0 21.4 %all-to-all-start.1 = ((bf16[16,1,64,512]{3,2,1,0:T(8,128)(2,1)}), bf16[16,1,64,512]{3,2,1,0:T(8,128)(2,1)S(1)}, u32[]{:S(2)}, u32[]{:S(2)}) async-start(bf16[16,1,64,512]{3,2,1,0:T(8,128)(2,1)} %bitcast.19), calls=%async_computation.1 | async-start | bytes 2097152 | tf_op jit(solution)/shard_map/all_to_all | solution.py:90
  45.4 10.4 %copy-start.3 = (bf16[16,1,64,512]{3,2,1,0:T(8,128)(2,1)}, bf16[16,1,64,512]{3,2,1,0:T(8,128)(2,1)S(1)}, u32[]{:S(2)}) copy-start(bf16[16,1,64,512]{3,2,1,0:T(8,128)(2,1)S(1)} %all-to-all-done.1) | copy-start | bytes 3145732
  45.4 22.4 %all-to-all-start.2 = ((bf16[16,1,64,512]{3,2,1,0:T(8,128)(2,1)}), bf16[16,1,64,512]{3,2,1,0:T(8,128)(2,1)}, u32[]{:S(2)}, u32[]{:S(2)}) async-start(bf16[16,1,64,512]{3,2,1,0:T(8,128)(2,1)} %bitcast.23), calls=%async_computation.2 | async-start | bytes 2097152 | tf_op jit(solution)/shard_map/all_to_all | solution.py:91
  141.5 9.8 %copy-start.1 = (pred[8,64,1024]{2,1,0:T(8,128)(4,1)S(1)}, pred[8,64,1024]{2,1,0:T(8,128)(4,1)}, u32[]{:S(2)}) copy-start(pred[8,64,1024]{2,1,0:T(8,128)(4,1)} %or_and_fusion.2) | copy-start | bytes 1572868 | tf_op jit(solution)/shard_map/while
  141.5 22.3 %slice-start = ((s8[8388608]{0:T(1024)(128)(4,1)}), s8[4194304]{0:T(1024)(128)(4,1)S(1)}, s32[]{:S(2)}) async-start(s8[8388608]{0:T(1024)(128)(4,1)} %bitcast.120), calls=%async_computation.8 | async-start | bytes 8388608 | tf_op jit(solution)/shard_map/while
  151.3 12.6 %slice-start.1 = ((s8[8388608]{0:T(1024)(128)(4,1)}), s8[4194304]{0:T(1024)(128)(4,1)S(1)}, s32[]{:S(2)}) async-start(s8[8388608]{0:T(1024)(128)(4,1)} %bitcast.120), calls=%async_computation.9 | async-start | bytes 8388608 | tf_op jit(solution)/shard_map/while
  151.3 12.6 %copy-start = (f32[8,4,64,128]{3,1,2,0:T(4,128)S(1)}, f32[8,4,64,128]{3,1,2,0:T(4,128)}, u32[]{:S(2)}) copy-start(f32[8,4,64,128]{3,1,2,0:T(4,128)} %bitcast_convert_fusion.2) | copy-start | bytes 3145732 | tf_op jit(solution)/shard_map/while
  416.3 9.8 %copy-start.1 = (pred[8,64,1024]{2,1,0:T(8,128)(4,1)S(1)}, pred[8,64,1024]{2,1,0:T(8,128)(4,1)}, u32[]{:S(2)}) copy-start(pred[8,64,1024]{2,1,0:T(8,128)(4,1)} %or_and_fusion.2) | copy-start | bytes 1572868 | tf_op jit(solution)/shard_map/while
  416.3 22.3 %slice-start = ((s8[8388608]{0:T(1024)(128)(4,1)}), s8[4194304]{0:T(1024)(128)(4,1)S(1)}, s32[]{:S(2)}) async-start(s8[8388608]{0:T(1024)(128)(4,1)} %bitcast.120), calls=%async_computation.8 | async-start | bytes 8388608 | tf_op jit(solution)/shard_map/while
  426.1 12.6 %slice-start.1 = ((s8[8388608]{0:T(1024)(128)(4,1)}), s8[4194304]{0:T(1024)(128)(4,1)S(1)}, s32[]{:S(2)}) async-start(s8[8388608]{0:T(1024)(128)(4,1)} %bitcast.120), calls=%async_computation.9 | async-start | bytes 8388608 | tf_op jit(solution)/shard_map/while
  426.1 12.6 %copy-start = (f32[8,4,64,128]{3,1,2,0:T(4,128)S(1)}, f32[8,4,64,128]{3,1,2,0:T(4,128)}, u32[]{:S(2)}) copy-start(f32[8,4,64,128]{3,1,2,0:T(4,128)} %bitcast_convert_fusion.2) | copy-start | bytes 3145732 | tf_op jit(solution)/shard_map/while
  643.5 20.0 %all-to-all-start.3 = ((bf16[8,128,512]{2,1,0:T(8,128)(2,1)}), bf16[8,128,512]{2,1,0:T(8,128)(2,1)S(1)}, u32[]{:S(2)}, u32[]{:S(2)}) async-start(bf16[8,128,512]{2,1,0:T(8,128)(2,1)} %bitcast.132), calls=%async_computation.3 | async-start | bytes 2097152 | tf_op jit(solution)/shard_map/all_to_all | solution.py:145
  663.5 46.0 %copy-start.5 = (s32[16]{0:T(128)S(1)}, s32[16]{0:T(128)}, u32[]{:S(2)}) copy-start(s32[16]{0:T(128)} %get-tuple-element.154) | copy-start | bytes 196
  663.5 38.9 %all-to-all-start.4 = ((f32[16,1,64,512]{3,2,1,0:T(8,128)}), f32[16,1,64,512]{3,2,1,0:T(8,128)}, u32[]{:S(2)}, u32[]{:S(2)}) async-start(f32[16,1,64,512]{3,2,1,0:T(8,128)} %get-tuple-element.188), calls=%async_computation.4 | async-start | bytes 4194304 | tf_op jit(solution)/shard_map/all_to_all | solution.py:122
  702.4 35.7 %all-to-all-start.6 = ((f32[16,1,64,512]{3,2,1,0:T(8,128)}), f32[16,1,64,512]{3,2,1,0:T(8,128)}, u32[]{:S(2)}, u32[]{:S(2)}) async-start(f32[16,1,64,512]{3,2,1,0:T(8,128)} %get-tuple-element.186), calls=%async_computation.6 | async-start | bytes 4194304 | tf_op jit(solution)/shard_map/all_to_all | solution.py:129
  738.1 20.1 %all-to-all-start.5 = ((bf16[8,128,512]{2,1,0:T(8,128)(2,1)}), bf16[8,128,512]{2,1,0:T(8,128)(2,1)}, u32[]{:S(2)}, u32[]{:S(2)}) async-start(bf16[8,128,512]{2,1,0:T(8,128)(2,1)} %bitcast_dynamic-update-slice_fusion), calls=%async_computation.5 | async-start | bytes 2097152 | tf_op jit(solution)/shard_map/all_to_all | solution.py:147
  758.2 19.3 %all-to-all-start.7 = ((bf16[8,128,512]{2,1,0:T(8,128)(2,1)}), bf16[8,128,512]{2,1,0:T(8,128)(2,1)S(1)}, u32[]{:S(2)}, u32[]{:S(2)}) async-start(bf16[8,128,512]{2,1,0:T(8,128)(2,1)} %bitcast.43), calls=%async_computation.7 | async-start | bytes 2097152 | tf_op jit(solution)/shard_map/all_to_all | solution.py:152
